TPU v7x, 32 devices: a whole 2x2x4 slice. The times are simulated.
32 devices in a mesh: rep: 8 (over z, y), fsdp: 2 (over x), ctx: 2 (over core).
Axes of the slice: x: 2, y: 2, z: 4, core: 2. Of those that a mesh axis runs over, the one named last changes fastest.
Arguments:
- tokens: bfloat16 [32, 1024, 1280], P(('rep', 'fsdp'), 'ctx'), may hold values from -6 to 6
- prefixes: int32 [32], P(('rep', 'fsdp')), may hold values from 102 to 512, as said below
- query_weight: bfloat16 [1280, 1280], P(('fsdp', 'ctx')), may hold values from -0.15625 to 0.15625
- key_weight: bfloat16 [1280, 1280], P(('fsdp', 'ctx')), may hold values from -0.15625 to 0.15625
- value_weight: bfloat16 [1280, 1280], P(('fsdp', 'ctx')), may hold values from -0.15625 to 0.15625
- output_weight: bfloat16 [1280, 1280], P(('fsdp', 'ctx')), may hold values from -2 to 2
- up_weight: bfloat16 [1280, 1280], P(('fsdp', 'ctx')), may hold values from -0.15625 to 0.15625
- up_bias: float32 [1280], replicated, may hold values from -3 to 3
- down_weight: bfloat16 [1280, 1280], P(('fsdp', 'ctx')), may hold values from -0.15625 to 0.15625
- down_bias: float32 [1280], replicated, may hold values from -3 to 3
- attn_gain: float32 [1280], replicated, may hold values from 0.5 to 1.5
- mlp_gain: float32 [1280], replicated, may hold values from 0.5 to 1.5
- query_scale: float32 [80], replicated, may hold values from -2.5 to 2.5
- cotangent: bfloat16 [32, 1024, 1280], P(('rep', 'fsdp'), 'ctx'), may hold values from -6 to 6
Outputs:
- mixed: bfloat16 [32, 1024, 1280], P(('rep', 'fsdp'), 'ctx')
- tokens_grad: bfloat16 [32, 1024, 1280], P(('rep', 'fsdp'), 'ctx')
- query_grad: float32 [1280, 1280], P(('fsdp', 'ctx'))
- key_grad: float32 [1280, 1280], P(('fsdp', 'ctx'))
- value_grad: float32 [1280, 1280], P(('fsdp', 'ctx'))
- output_grad: float32 [1280, 1280], P(('fsdp', 'ctx'))
- up_grad: float32 [1280, 1280], P(('fsdp', 'ctx'))
- upbias_grad: float32 [1280], replicated
- down_grad: float32 [1280, 1280], P(('fsdp', 'ctx'))
- downbias_grad: float32 [1280], replicated
- attngain_grad: float32 [1280], replicated
- mlpgain_grad: float32 [1280], replicated
- scale_grad: float32 [80], replicated
Inputs may be any that keep to these rules, and one draw needn't show every extreme that they name: `prefixes`: at least one sequence has 1024 // 10 and one has 1024 // 2.
All inputs are finite; a program needn't handle non-finite values.
Results may differ from a plain program's by a relative error of at most 0.02.
Values may be sent and summed in bfloat16 or wider, within the bound.
No kernel may reach another device: no remote copies, remote signals or barrier semaphores. Data moves between devices by JAX's collectives and lax.ppermute only.
A program may use at most 384 MiB of HBM per device.

v0:
```python
import jax
import jax.numpy as jnp
from jax import lax
from jax.sharding import PartitionSpec as P

HD = 80
epsilon = 1e-06
softplus_gain = 1.442695041
masked_value = -1e30


def norm_factor(values):
    return lax.rsqrt(jnp.mean(values * values, axis=-1, keepdims=True) + epsilon)


def norm_back(upstream, values, factor, gain_vec):
    scaled = upstream * gain_vec
    row_inner = jnp.mean(scaled * values, axis=-1, keepdims=True)
    return factor * scaled - values * factor**3 * row_inner


def allowed_mask(offset, local_rows, length, prefix):
    row_index = offset + jnp.arange(local_rows, dtype=jnp.int32)[:, None]
    col_index = jnp.arange(length, dtype=jnp.int32)[None, :]
    return (col_index <= row_index) | (col_index < prefix)


def masked_scores(queries, keys, allowed):
    scores = jnp.einsum("qhe,khe->hqk", queries, keys, preferred_element_type=jnp.float32)
    return jnp.where(allowed[None], scores, masked_value)


def shards(
    tokens,
    prefixes,
    query_weight,
    key_weight,
    value_weight,
    output_weight,
    up_weight,
    up_bias,
    down_weight,
    down_bias,
    attn_gain,
    mlp_gain,
    query_scale,
    cotangent,
):
    seq_count, local_rows, model_width = tokens.shape
    head_count = model_width // HD
    position_index = lax.axis_index("ctx")
    offset = position_index * local_rows
    full_query, full_key, full_value, full_output, full_up, full_down = (
        lax.all_gather(query_weight, ("fsdp", "ctx"), axis=0, tiled=True),
        lax.all_gather(key_weight, ("fsdp", "ctx"), axis=0, tiled=True),
        lax.all_gather(value_weight, ("fsdp", "ctx"), axis=0, tiled=True),
        lax.all_gather(output_weight, ("fsdp", "ctx"), axis=0, tiled=True),
        lax.all_gather(up_weight, ("fsdp", "ctx"), axis=0, tiled=True),
        lax.all_gather(down_weight, ("fsdp", "ctx"), axis=0, tiled=True),
    )
    rows_in = tokens.reshape(seq_count * local_rows, model_width).astype(jnp.float32)
    factor_one = norm_factor(rows_in)
    normed = (rows_in * factor_one * attn_gain).astype(jnp.bfloat16)
    scale_soft = jax.nn.softplus(query_scale) * (softplus_gain * HD ** (-0.5))
    query_raw = jnp.dot(normed, full_query, preferred_element_type=jnp.float32).reshape(
        seq_count, local_rows, head_count, HD
    )
    queries = (query_raw * scale_soft).astype(jnp.bfloat16)
    key_local = (
        jnp.dot(normed, full_key, preferred_element_type=jnp.float32)
        .astype(jnp.bfloat16)
        .reshape(seq_count, local_rows, model_width)
    )
    value_local = (
        jnp.dot(normed, full_value, preferred_element_type=jnp.float32)
        .astype(jnp.bfloat16)
        .reshape(seq_count, local_rows, model_width)
    )
    key_all, value_all = (
        lax.all_gather(key_local, "ctx", axis=1, tiled=True),
        lax.all_gather(value_local, "ctx", axis=1, tiled=True),
    )
    length = key_all.shape[1]

    def forward_one(members):
        queries_seq, keys_seq, values_seq, prefix = members
        allowed = allowed_mask(offset, local_rows, length, prefix)
        scores = masked_scores(queries_seq, keys_seq.reshape(length, head_count, HD), allowed)
        row_max = jnp.max(scores, axis=-1, keepdims=True)
        weights = jnp.exp(scores - row_max)
        row_total = jnp.sum(weights, axis=-1, keepdims=True)
        probability = (weights / row_total).astype(jnp.bfloat16)
        context = jnp.einsum(
            "hqk,khe->qhe",
            probability,
            values_seq.reshape(length, head_count, HD),
            preferred_element_type=jnp.float32,
        )
        return (context, row_max + jnp.log(row_total))

    context, logsum = lax.map(forward_one, (queries, key_all, value_all, prefixes))
    attended = context.reshape(seq_count * local_rows, model_width).astype(jnp.bfloat16)
    middle = rows_in + jnp.dot(attended, full_output, preferred_element_type=jnp.float32)
    factor_two = norm_factor(middle)
    normed_two = (middle * factor_two * mlp_gain).astype(jnp.bfloat16)
    before = jnp.dot(normed_two, full_up, preferred_element_type=jnp.float32) + up_bias
    hidden = jax.nn.silu(before).astype(jnp.bfloat16)
    mixed_rows = middle + jnp.dot(hidden, full_down, preferred_element_type=jnp.float32) + down_bias
    mixed_out = mixed_rows.astype(jnp.bfloat16).reshape(seq_count, local_rows, model_width)
    key_back, value_back = (key_all, value_all)
    back_query, back_key, back_value, back_output, back_up, back_down = (
        lax.all_gather(query_weight, ("fsdp", "ctx"), axis=0, tiled=True),
        lax.all_gather(key_weight, ("fsdp", "ctx"), axis=0, tiled=True),
        lax.all_gather(value_weight, ("fsdp", "ctx"), axis=0, tiled=True),
        lax.all_gather(output_weight, ("fsdp", "ctx"), axis=0, tiled=True),
        lax.all_gather(up_weight, ("fsdp", "ctx"), axis=0, tiled=True),
        lax.all_gather(down_weight, ("fsdp", "ctx"), axis=0, tiled=True),
    )
    key_back, value_back = (
        lax.all_gather(key_local, "ctx", axis=1, tiled=True),
        lax.all_gather(value_local, "ctx", axis=1, tiled=True),
    )
    upstream = cotangent.reshape(seq_count * local_rows, model_width)
    upstream_wide = upstream.astype(jnp.float32)
    down_part = jnp.einsum("nf,nd->fd", hidden, upstream, preferred_element_type=jnp.float32)
    downbias_part = jnp.sum(upstream_wide, axis=0)
    hidden_grad = jnp.einsum("nd,fd->nf", upstream, back_down, preferred_element_type=jnp.float32)
    gate_sig = jax.nn.sigmoid(before)
    before_grad = (hidden_grad * gate_sig * (1.0 + before * (1.0 - gate_sig))).astype(jnp.bfloat16)
    up_part = jnp.einsum("nd,nf->df", normed_two, before_grad, preferred_element_type=jnp.float32)
    upbias_part = jnp.sum(before_grad.astype(jnp.float32), axis=0)
    normed_grad = jnp.einsum("nf,df->nd", before_grad, back_up, preferred_element_type=jnp.float32)
    mlpgain_part = jnp.sum(normed_grad * middle * factor_two, axis=0)
    middle_grad = upstream_wide + norm_back(normed_grad, middle, factor_two, mlp_gain)
    middle_low = middle_grad.astype(jnp.bfloat16)
    output_part = jnp.einsum("nd,ne->de", attended, middle_low, preferred_element_type=jnp.float32)
    context_grad = jnp.einsum(
        "ne,de->nd", middle_low, back_output, preferred_element_type=jnp.float32
    )
    context_grad = context_grad.astype(jnp.bfloat16).reshape(seq_count, local_rows, head_count, HD)

    def backward_one(members):
        queries_seq, keys_seq, values_seq, grad_seq, logsum_seq, prefix = members
        keys_heads = keys_seq.reshape(length, head_count, HD)
        values_heads = values_seq.reshape(length, head_count, HD)
        allowed = allowed_mask(offset, local_rows, length, prefix)
        scores = masked_scores(queries_seq, keys_heads, allowed)
        exact_prob = jnp.exp(scores - logsum_seq)
        probability = exact_prob.astype(jnp.bfloat16)
        prob_grad = jnp.einsum(
            "qhe,khe->hqk", grad_seq, values_heads, preferred_element_type=jnp.float32
        )
        row_inner = jnp.sum(prob_grad * exact_prob, axis=-1, keepdims=True)
        score_grad = (exact_prob * (prob_grad - row_inner)).astype(jnp.bfloat16)
        query_part = jnp.einsum(
            "hqk,khe->qhe", score_grad, keys_heads, preferred_element_type=jnp.float32
        )
        key_term = jnp.einsum(
            "hqk,qhe->khe", score_grad, queries_seq, preferred_element_type=jnp.float32
        )
        value_term = jnp.einsum(
            "hqk,qhe->khe", probability, grad_seq, preferred_element_type=jnp.float32
        )
        return (
            query_part,
            key_term.reshape(length, model_width),
            value_term.reshape(length, model_width),
        )

    query_seqgrad, key_partial, value_partial = lax.map(
        backward_one, (queries, key_back, value_back, context_grad, logsum, prefixes)
    )
    key_summed, value_summed = (
        lax.psum_scatter(key_partial, "ctx", scatter_dimension=1, tiled=True),
        lax.psum_scatter(value_partial, "ctx", scatter_dimension=1, tiled=True),
    )
    key_low = key_summed.astype(jnp.bfloat16).reshape(seq_count * local_rows, model_width)
    value_low = value_summed.astype(jnp.bfloat16).reshape(seq_count * local_rows, model_width)
    scaled_low = query_seqgrad.astype(jnp.bfloat16)
    query_low = (
        (scaled_low * scale_soft).astype(jnp.bfloat16).reshape(seq_count * local_rows, model_width)
    )
    scale_part = jnp.sum(scaled_low * query_raw, axis=(0, 1, 2))
    scale_part = scale_part * jax.nn.sigmoid(query_scale) * (softplus_gain * HD ** (-0.5))
    query_part = jnp.einsum("nd,ne->de", normed, query_low, preferred_element_type=jnp.float32)
    key_part = jnp.einsum("nd,ne->de", normed, key_low, preferred_element_type=jnp.float32)
    value_part = jnp.einsum("nd,ne->de", normed, value_low, preferred_element_type=jnp.float32)
    normed_grad_one = jnp.einsum(
        "ne,de->nd", query_low, back_query, preferred_element_type=jnp.float32
    )
    normed_grad_one = normed_grad_one + jnp.einsum(
        "ne,de->nd", key_low, back_key, preferred_element_type=jnp.float32
    )
    normed_grad_one = normed_grad_one + jnp.einsum(
        "ne,de->nd", value_low, back_value, preferred_element_type=jnp.float32
    )
    attngain_part = jnp.sum(normed_grad_one * rows_in * factor_one, axis=0)
    tokens_grad = middle_grad + norm_back(normed_grad_one, rows_in, factor_one, attn_gain)
    tokens_grad = tokens_grad.astype(jnp.bfloat16).reshape(seq_count, local_rows, model_width)
    query_shard, key_shard, value_shard, output_shard, up_shard, down_shard = (
        lax.psum_scatter(
            query_part.astype(jnp.bfloat16), ("fsdp", "ctx"), scatter_dimension=0, tiled=True
        ).astype(jnp.float32),
        lax.psum_scatter(
            key_part.astype(jnp.bfloat16), ("fsdp", "ctx"), scatter_dimension=0, tiled=True
        ).astype(jnp.float32),
        lax.psum_scatter(
            value_part.astype(jnp.bfloat16), ("fsdp", "ctx"), scatter_dimension=0, tiled=True
        ).astype(jnp.float32),
        lax.psum_scatter(
            output_part.astype(jnp.bfloat16), ("fsdp", "ctx"), scatter_dimension=0, tiled=True
        ).astype(jnp.float32),
        lax.psum_scatter(
            up_part.astype(jnp.bfloat16), ("fsdp", "ctx"), scatter_dimension=0, tiled=True
        ).astype(jnp.float32),
        lax.psum_scatter(
            down_part.astype(jnp.bfloat16), ("fsdp", "ctx"), scatter_dimension=0, tiled=True
        ).astype(jnp.float32),
    )
    query_total, key_total, value_total, output_total, up_total, down_total = (
        lax.psum(query_shard.astype(jnp.bfloat16), "rep").astype(jnp.float32),
        lax.psum(key_shard.astype(jnp.bfloat16), "rep").astype(jnp.float32),
        lax.psum(value_shard.astype(jnp.bfloat16), "rep").astype(jnp.float32),
        lax.psum(output_shard.astype(jnp.bfloat16), "rep").astype(jnp.float32),
        lax.psum(up_shard.astype(jnp.bfloat16), "rep").astype(jnp.float32),
        lax.psum(down_shard.astype(jnp.bfloat16), "rep").astype(jnp.float32),
    )
    upbias_total, downbias_total, attngain_total, mlpgain_total, scale_total = lax.psum(
        (upbias_part, downbias_part, attngain_part, mlpgain_part, scale_part),
        ("rep", "fsdp", "ctx"),
    )
    return (
        mixed_out,
        tokens_grad,
        query_total,
        key_total,
        value_total,
        output_total,
        up_total,
        upbias_total,
        down_total,
        downbias_total,
        attngain_total,
        mlpgain_total,
        scale_total,
    )


def solution(mesh):
    return jax.shard_map(
        shards,
        mesh=mesh,
        in_specs=(
            P(("rep", "fsdp"), "ctx", None),
            P(("rep", "fsdp")),
            P(("fsdp", "ctx"), None),
            P(("fsdp", "ctx"), None),
            P(("fsdp", "ctx"), None),
            P(("fsdp", "ctx"), None),
            P(("fsdp", "ctx"), None),
            P(),
            P(("fsdp", "ctx"), None),
            P(),
            P(),
            P(),
            P(),
            P(("rep", "fsdp"), "ctx", None),
        ),
        out_specs=(
            P(("rep", "fsdp"), "ctx", None),
            P(("rep", "fsdp"), "ctx", None),
            P(("fsdp", "ctx"), None),
            P(("fsdp", "ctx"), None),
            P(("fsdp", "ctx"), None),
            P(("fsdp", "ctx"), None),
            P(("fsdp", "ctx"), None),
            P(),
            P(("fsdp", "ctx"), None),
            P(),
            P(),
            P(),
            P(),
        ),
        check_vma=False,
    )
```

profile of v0, /device:TPU:0, one launch (start us, length us, event | category | flops | bytes accessed | tf_op | source)
XLA Modules:
  0.0 1070.1 jit_solution(11149948379400811405)
XLA Ops:
  15.3 26.3 %all-gather.15.cloned.1.call-done = bf16[1280,1280]{1,0:T(8,128)(2,1)} async-done(((bf16[320,1280]{1,0:T(8,128)(2,1)}), bf16[1280,1280]{1,0:T(8,128)(2,1)}) %all-gather.15.cloned.1.call-update) | async-done | bytes 3276816 | tf_op jit(solution)/shard_map/all_gather | solution.py:55
  41.6 7.8 convolution_convert_fusion.5
  49.3 4.5 copy.37
  53.9 18.5 %all-gather.9.cloned.1.call-done = bf16[1280,1280]{1,0:T(8,128)(2,1)} async-done(((bf16[320,1280]{1,0:T(8,128)(2,1)}), bf16[1280,1280]{1,0:T(8,128)(2,1)}) %all-gather.9.cloned.1.call-update) | async-done | bytes 3276816 | tf_op jit(solution)/shard_map/all_gather | solution.py:56
  72.4 7.8 convolution_convert_fusion.6
  80.2 4.5 copy.35
  89.3 14.0 %all-gather.13.cloned.1.call-done = bf16[1280,1280]{1,0:T(8,128)(2,1)} async-done(((bf16[320,1280]{1,0:T(8,128)(2,1)}), bf16[1280,1280]{1,0:T(8,128)(2,1)}) %all-gather.13.cloned.1.call-update) | async-done | bytes 3276816 | tf_op jit(solution)/shard_map/all_gather | solution.py:54
  103.3 5.6 copy.36
  108.9 9.2 multiply_convert_fusion.4
  119.9 18.4 %all-gather.11.cloned.1.call-done = bf16[2,1024,1280]{1,2,0:T(8,128)(2,1)} async-done(((bf16[2,512,1280]{1,2,0:T(8,128)(2,1)}), bf16[2,1024,1280]{1,2,0:T(8,128)(2,1)}) %all-gather.11.cloned.1.call-update) | async-done | bytes 5242896 | tf_op jit(solution)/shard_map/all_gather | solution.py:81
  140.1 103.8 %while.26 = (s32[]{:T(128)}, bf16[2,512,16,80]{1,3,2,0:T(8,128)(2,1)}, f32[2,16,512,1]{2,1,3,0:T(8,128)S(1)}, bf16[2,1024,1280]{1,2,0:T(8,128)(2,1)}, s32[]{:T(1...) while((s32[]{:T(128)}, ...), condition=%wide.region_4.5_spmd, body=%wide.region_1.4_spmd.sunk | while | flops 2760893952 | bytes 154147024 | solution.py:101
  141.7 4.6 constant_dynamic-slice_fusion.7
  146.4 13.5 %select_reduce_fusion.2 = (f32[16,512]{1,0:T(8,128)S(1)}, f32[16,512,1024]{2,1,0:T(8,128)}) fusion(pred[512,1024]{1,0:T(8,128)(4,1)S(1)} %fusion.112, bf16[1024,16,80]{0,2,1:T(8,128)(2,1)S(1)} %bitcast.193, bf16[2,512,16,80]{1,3,2,0:T(8,128)(2,1)S(1)} %get-tuple-element.373, s32[]{:T(128)S(6)} %copy.79), kind=kOutput, calls=%fused_computation.2.clone.1 | convolution fusion | flops 1358946304 | bytes 38043652 | tf_op jit(solution)/shard_map/while/body/eval_jaxpr/qhe,khe->hqk/dot_general | solution.py:29
  159.9 15.4 %fusion.113 = f32[16,512]{1,0:T(8,128)S(1)} fusion(f32[16,512,1024]{2,1,0:T(8,128)} %get-tuple-element.332, f32[16,512]{1,0:T(8,128)S(1)} %get-tuple-element.333, pred[512,1024]{1,0:T(8,128)(4,1)S(1)} %fusion.112), kind=kLoop, calls=%fused_computation.3.clone.1 | loop fusion | flops 25157632 | bytes 34144256 | tf_op jit(solution)/shard_map/while/body/eval_jaxpr/reduce_sum | solution.py:91
  175.3 15.2 %bitcast_dynamic-update-slice_fusion.6 = bf16[2,512,16,80]{1,3,2,0:T(8,128)(2,1)S(1)} fusion(bf16[2,512,16,80]{1,3,2,0:T(8,128)(2,1)S(1)} %copy-done.8, s32[]{:T(128)S(6)} %copy.79, bf16[1024,16,80]{0,2,1:T(8,128)(2,1)S(1)} %bitcast.196, f32[16,512,1024]{2,1,0:T(8,128)} %get-tuple-element.332, f32[16,512]{1,0:T(8,128)S(1)} %fusion.113, ...), kind=kOutput, calls=%fused_computation.5.clone.1 | convolution fusion | flops 1375731712 | bytes 39387140 | tf_op jit(solution)/shard_map/while/body/eval_jaxpr/hqk,khe->qhe/dot_general | solution.py:93
  193.6 4.6 constant_dynamic-slice_fusion.7
  198.3 14.3 %select_reduce_fusion.2 = (f32[16,512]{1,0:T(8,128)S(1)}, f32[16,512,1024]{2,1,0:T(8,128)}) fusion(pred[512,1024]{1,0:T(8,128)(4,1)S(1)} %fusion.112, bf16[1024,16,80]{0,2,1:T(8,128)(2,1)S(1)} %bitcast.193, bf16[2,512,16,80]{1,3,2,0:T(8,128)(2,1)S(1)} %get-tuple-element.373, s32[]{:T(128)S(6)} %copy.79), kind=kOutput, calls=%fused_computation.2.clone.1 | convolution fusion | flops 1358946304 | bytes 38043652 | tf_op jit(solution)/shard_map/while/body/eval_jaxpr/qhe,khe->hqk/dot_general | solution.py:29
  212.6 15.3 %fusion.113 = f32[16,512]{1,0:T(8,128)S(1)} fusion(f32[16,512,1024]{2,1,0:T(8,128)} %get-tuple-element.332, f32[16,512]{1,0:T(8,128)S(1)} %get-tuple-element.333, pred[512,1024]{1,0:T(8,128)(4,1)S(1)} %fusion.112), kind=kLoop, calls=%fused_computation.3.clone.1 | loop fusion | flops 25157632 | bytes 34144256 | tf_op jit(solution)/shard_map/while/body/eval_jaxpr/reduce_sum | solution.py:91
  228.0 14.3 %bitcast_dynamic-update-slice_fusion.6 = bf16[2,512,16,80]{1,3,2,0:T(8,128)(2,1)S(1)} fusion(bf16[2,512,16,80]{1,3,2,0:T(8,128)(2,1)S(1)} %copy-done.8, s32[]{:T(128)S(6)} %copy.79, bf16[1024,16,80]{0,2,1:T(8,128)(2,1)S(1)} %bitcast.196, f32[16,512,1024]{2,1,0:T(8,128)} %get-tuple-element.332, f32[16,512]{1,0:T(8,128)S(1)} %fusion.113, ...), kind=kOutput, calls=%fused_computation.5.clone.1 | convolution fusion | flops 1375731712 | bytes 39387140 | tf_op jit(solution)/shard_map/while/body/eval_jaxpr/hqk,khe->qhe/dot_general | solution.py:93
  250.6 9.7 multiply_reduce_fusion.3
  260.3 9.4 fusion.54
  269.7 10.1 convert_reduce_fusion.1
  279.8 4.5 multiply_reduce_fusion.1
  288.6 4.9 convolution_convert_fusion.4
  293.4 8.5 reshape.299
  302.0 7.2 copy.40
  311.0 272.4 %while.27 = (s32[]{:T(128)}, bf16[2,512,16,80]{1,3,2,0:T(8,128)(2,1)}, f32[2,1024,1280]{2,1,0:T(8,128)}, f32[2,1024,1280]{2,1,0:T(8,128)}, bf16[2,1024,1280]{1,2...) while((s32[]{:T(128)}, ...), condition=%wide.region_9.10_spmd, body=%wide.region_7.9_spmd.sunk | while | flops 6812591616 | bytes 374577376 | solution.py:170
  317.9 14.5 %fusion.123 = f32[16,512,1024]{2,1,0:T(8,128)} fusion(bf16[1024,16,80]{0,2,1:T(8,128)(2,1)S(1)} %bitcast.190, bf16[2,512,16,80]{1,3,2,0:T(8,128)(2,1)} %copy-done, s32[]{:T(128)S(6)} %copy.89), kind=kOutput, calls=%fused_computation.34.clone.1 | convolution fusion | flops 1342177280 | bytes 37486596 | tf_op jit(solution)/shard_map/while/body/eval_jaxpr/qhe,khe->hqk/dot_general | solution.py:29
  332.4 17.1 %fusion.125 = f32[16,80,1024]{2,1,0:T(8,128)} fusion(f32[16,512,1024]{2,1,0:T(8,128)} %fusion.123, f32[16,512]{1,0:T(8,128)S(1)} %dynamic-slice_bitcast_fusion.2, pred[512,1024]{1,0:T(8,128)(4,1)S(1)} %fusion.124, bf16[2,512,16,80]{1,3,2,0:T(8,128)(2,1)} %get-tuple-element.409, s32[]{:T(128)S(6)} %copy.89), kind=kOutput, calls=%fused_computation.22.clone.1 | convolution fusion | flops 1367343104 | bytes 40665092 | tf_op jit(solution)/shard_map/while/body/eval_jaxpr/hqk,qhe->khe/dot_general | solution.py:161
  349.5 5.9 copy.69
  355.4 25.5 %multiply_reduce_fusion.5 = (f32[16,512]{1,0:T(8,128)S(1)}, f32[16,512,1024]{2,1,0:T(8,128)}) fusion(f32[16,512,1024]{2,1,0:T(8,128)} %fusion.123, f32[16,512]{1,0:T(8,128)S(1)} %dynamic-slice_bitcast_fusion.2, pred[512,1024]{1,0:T(8,128)(4,1)S(1)} %fusion.124, bf16[1024,16,80]{0,2,1:T(8,128)(2,1)} %bitcast.195, ...), kind=kOutput, calls=%fused_computation.19.clone.1 | convolution fusion | flops 1375723520 | bytes 71630848 | tf_op jit(solution)/shard_map/while/body/eval_jaxpr/qhe,khe->hqk/dot_general | solution.py:150
  380.9 27.8 %multiply_convert_fusion.10 = bf16[16,512,1024]{2,1,0:T(8,128)(2,1)} fusion(f32[16,512,1024]{2,1,0:T(8,128)} %get-tuple-element.345, f32[16,512,1024]{2,1,0:T(8,128)} %fusion.123, f32[16,512]{1,0:T(8,128)S(1)} %get-tuple-element.346, f32[16,512]{1,0:T(8,128)S(1)} %dynamic-slice_bitcast_fusion.2, pred[512,1024]{1,0:T(8,128)(4,1)S(1)} %fusion.124), kind=kLoop, calls=%fused_computation.18.clone.1 | loop fusion | flops 41943040 | bytes 84475904 | tf_op jit(solution)/shard_map/while/body/eval_jaxpr/convert_element_type | solution.py:154
  408.7 12.1 %bitcast_dynamic-update-slice_fusion.8 = bf16[2,512,16,80]{1,3,2,0:T(8,128)(2,1)} fusion(bf16[2,512,16,80]{1,3,2,0:T(8,128)(2,1)} %get-tuple-element.389, s32[]{:T(128)S(6)} %copy.89, bf16[1024,16,80]{0,2,1:T(8,128)(2,1)S(1)} %bitcast.191, bf16[16,512,1024]{2,1,0:T(8,128)(2,1)} %multiply_convert_fusion.10), kind=kOutput, calls=%fused_computation.26.clone.1 | convolution fusion | flops 1342177280 | bytes 22020100 | tf_op jit(solution)/shard_map/while/body/eval_jaxpr/hqk,khe->qhe/dot_general | solution.py:155
  420.8 11.6 %fusion.126 = f32[16,80,1024]{2,1,0:T(8,128)} fusion(bf16[16,512,1024]{2,1,0:T(8,128)(2,1)} %multiply_convert_fusion.10, bf16[2,512,16,80]{1,3,2,0:T(8,128)(2,1)} %copy-done, s32[]{:T(128)S(6)} %copy.89), kind=kOutput, calls=%fused_computation.32.clone.1 | convolution fusion | flops 1342177280 | bytes 23330820 | tf_op jit(solution)/shard_map/while/body/eval_jaxpr/hqk,qhe->khe/dot_general | solution.py:158
  432.4 5.9 copy.70
  438.4 8.8 constant_dynamic-update-slice_fusion.3
  453.8 14.5 %fusion.123 = f32[16,512,1024]{2,1,0:T(8,128)} fusion(bf16[1024,16,80]{0,2,1:T(8,128)(2,1)S(1)} %bitcast.190, bf16[2,512,16,80]{1,3,2,0:T(8,128)(2,1)} %copy-done, s32[]{:T(128)S(6)} %copy.89), kind=kOutput, calls=%fused_computation.34.clone.1 | convolution fusion | flops 1342177280 | bytes 37486596 | tf_op jit(solution)/shard_map/while/body/eval_jaxpr/qhe,khe->hqk/dot_general | solution.py:29
  468.4 17.1 %fusion.125 = f32[16,80,1024]{2,1,0:T(8,128)} fusion(f32[16,512,1024]{2,1,0:T(8,128)} %fusion.123, f32[16,512]{1,0:T(8,128)S(1)} %dynamic-slice_bitcast_fusion.2, pred[512,1024]{1,0:T(8,128)(4,1)S(1)} %fusion.124, bf16[2,512,16,80]{1,3,2,0:T(8,128)(2,1)} %get-tuple-element.409, s32[]{:T(128)S(6)} %copy.89), kind=kOutput, calls=%fused_computation.22.clone.1 | convolution fusion | flops 1367343104 | bytes 40665092 | tf_op jit(solution)/shard_map/while/body/eval_jaxpr/hqk,qhe->khe/dot_general | solution.py:161
  485.5 5.9 copy.69
  491.3 25.5 %multiply_reduce_fusion.5 = (f32[16,512]{1,0:T(8,128)S(1)}, f32[16,512,1024]{2,1,0:T(8,128)}) fusion(f32[16,512,1024]{2,1,0:T(8,128)} %fusion.123, f32[16,512]{1,0:T(8,128)S(1)} %dynamic-slice_bitcast_fusion.2, pred[512,1024]{1,0:T(8,128)(4,1)S(1)} %fusion.124, bf16[1024,16,80]{0,2,1:T(8,128)(2,1)} %bitcast.195, ...), kind=kOutput, calls=%fused_computation.19.clone.1 | convolution fusion | flops 1375723520 | bytes 71630848 | tf_op jit(solution)/shard_map/while/body/eval_jaxpr/qhe,khe->hqk/dot_general | solution.py:150
  516.8 27.8 %multiply_convert_fusion.10 = bf16[16,512,1024]{2,1,0:T(8,128)(2,1)} fusion(f32[16,512,1024]{2,1,0:T(8,128)} %get-tuple-element.345, f32[16,512,1024]{2,1,0:T(8,128)} %fusion.123, f32[16,512]{1,0:T(8,128)S(1)} %get-tuple-element.346, f32[16,512]{1,0:T(8,128)S(1)} %dynamic-slice_bitcast_fusion.2, pred[512,1024]{1,0:T(8,128)(4,1)S(1)} %fusion.124), kind=kLoop, calls=%fused_computation.18.clone.1 | loop fusion | flops 41943040 | bytes 84475904 | tf_op jit(solution)/shard_map/while/body/eval_jaxpr/convert_element_type | solution.py:154
  544.7 12.0 %bitcast_dynamic-update-slice_fusion.8 = bf16[2,512,16,80]{1,3,2,0:T(8,128)(2,1)} fusion(bf16[2,512,16,80]{1,3,2,0:T(8,128)(2,1)} %get-tuple-element.389, s32[]{:T(128)S(6)} %copy.89, bf16[1024,16,80]{0,2,1:T(8,128)(2,1)S(1)} %bitcast.191, bf16[16,512,1024]{2,1,0:T(8,128)(2,1)} %multiply_convert_fusion.10), kind=kOutput, calls=%fused_computation.26.clone.1 | convolution fusion | flops 1342177280 | bytes 22020100 | tf_op jit(solution)/shard_map/while/body/eval_jaxpr/hqk,khe->qhe/dot_general | solution.py:155
  556.7 11.6 %fusion.126 = f32[16,80,1024]{2,1,0:T(8,128)} fusion(bf16[16,512,1024]{2,1,0:T(8,128)(2,1)} %multiply_convert_fusion.10, bf16[2,512,16,80]{1,3,2,0:T(8,128)(2,1)} %copy-done, s32[]{:T(128)S(6)} %copy.89), kind=kOutput, calls=%fused_computation.32.clone.1 | convolution fusion | flops 1342177280 | bytes 23330820 | tf_op jit(solution)/shard_map/while/body/eval_jaxpr/hqk,qhe->khe/dot_general | solution.py:158
  568.3 5.9 copy.70
  574.2 8.7 constant_dynamic-update-slice_fusion.3
  585.2 9.0 convolution_convert_fusion
  594.3 11.4 %convolution_convert_fusion.1 = bf16[1280,1280]{1,0:T(8,128)(2,1)} fusion(bf16[1024,1280]{1,0:T(8,128)(2,1)} %copy-done.47, f32[1024,1280]{1,0:T(8,128)} %get-tuple-element.212, f32[1280]{0:T(1024)S(1)} %copy-done.32, f32[1024]{0:T(1024)S(1)} %copy-done.30), kind=kOutput, calls=%fused_computation.57 | convolution fusion | flops 3361013760 | bytes 11150336 | tf_op jit(solution)/shard_map/nd,nf->df/dot_general | solution.py:130
  605.8 7.4 convolution_convert_fusion.2
  613.5 6.3 fusion.34
  624.9 5.1 convolution_convert_fusion.3
  634.3 5.1 fusion.32
  643.7 7.7 fusion.31
  652.2 8.7 fusion.55
  660.9 6.0 reduce-scatter.23.cloned.1.call-done
  667.0 41.2 %reduce-scatter.21.cloned.1.call-done = bf16[320,1280]{1,0:T(8,128)(2,1)} async-done(((bf16[1280,1280]{1,0:T(8,128)(2,1)}), bf16[320,1280]{1,0:T(8,128)(2,1)}) %reduce-scatter.21.cloned.1.call-update) | async-done | bytes 819216 | tf_op jit(solution)/shard_map/reduce_scatter | solution.py:213
  708.1 41.3 %reduce-scatter.19.cloned.1.call-done = bf16[320,1280]{1,0:T(8,128)(2,1)} async-done(((bf16[1280,1280]{1,0:T(8,128)(2,1)}), bf16[320,1280]{1,0:T(8,128)(2,1)}) %reduce-scatter.19.cloned.1.call-update) | async-done | bytes 819216 | tf_op jit(solution)/shard_map/reduce_scatter | solution.py:210
  749.4 41.2 %reduce-scatter.13.cloned.1.call-done = bf16[320,1280]{1,0:T(8,128)(2,1)} async-done(((bf16[1280,1280]{1,0:T(8,128)(2,1)}), bf16[320,1280]{1,0:T(8,128)(2,1)}) %reduce-scatter.13.cloned.1.call-update) | async-done | bytes 819216 | tf_op jit(solution)/shard_map/reduce_scatter | solution.py:201
  790.6 41.1 %reduce-scatter.17.cloned.1.call-done = bf16[320,1280]{1,0:T(8,128)(2,1)} async-done(((bf16[1280,1280]{1,0:T(8,128)(2,1)}), bf16[320,1280]{1,0:T(8,128)(2,1)}) %reduce-scatter.17.cloned.1.call-update) | async-done | bytes 819216 | tf_op jit(solution)/shard_map/reduce_scatter | solution.py:207
  831.7 41.2 %reduce-scatter.15.cloned.1.call-done = bf16[320,1280]{1,0:T(8,128)(2,1)} async-done(((bf16[1280,1280]{1,0:T(8,128)(2,1)}), bf16[320,1280]{1,0:T(8,128)(2,1)}) %reduce-scatter.15.cloned.1.call-update) | async-done | bytes 819216 | tf_op jit(solution)/shard_map/reduce_scatter | solution.py:204
  872.9 10.9 %add_convert_fusion = bf16[1024,1280]{1,0:T(8,128)(2,1)} fusion(f32[1024,1280]{1,0:T(8,128)} %get-tuple-element.212, bf16[1280,1280]{1,0:T(8,128)(2,1)} %all-gather.23.cloned.1.call-done, f32[1280]{0:T(1024)S(1)} %copy-done.40, f32[1024,1280]{1,0:T(8,128)} %fusion.54, f32[1280]{0:T(1024)S(1)} %copy-done.42), kind=kOutput, calls=%fused_computation.90 | convolution fusion | flops 3367239680 | bytes 16394240 | tf_op jit(solution)/shard_map/dot_general | solution.py:108
  888.9 6.3 fusion.46
  895.2 46.5 %all-reduce = (f32[1280]{0:T(1024)}, f32[1280]{0:T(1024)}, f32[1280]{0:T(1024)}, f32[1280]{0:T(1024)}, f32[80]{0:T(128)}) all-reduce(f32[1280]{0:T(1024)S(1)} %copy-done.33, f32[1280]{0:T(1024)S(1)} %convert_reduce_fusion, f32[1280]{0:T(1024)S(1)} %get-tuple-element.144, ...), channel_id=1, replica_groups=mesh['rep'=8,'fsdp'=2,'ctx'=2] {'rep','fsdp','ctx'}, use_global_device_ids=true, to_apply=%region_24.25 | all-reduce | flops 5200 | bytes 41600 | tf_op jit(solution)/shard_map/psum | solution.py:228
  941.7 6.0 fusion.43
  947.7 105.4 %all-reduce.4.cloned.1.call-done = (bf16[320,1280]{1,0:T(8,128)(2,1)}, bf16[320,1280]{1,0:T(8,128)(2,1)}, bf16[320,1280]{1,0:T(8,128)(2,1)}, bf16[320,1280]{1,0:...) async-done(((bf16[320,1280]{1,0:T(8,128)(2,1)}, bf16[320,1280]{1,0:T(8,128)(2,1)}, bf16[320,1280]{1,0:T(8,128)(2,1)}, bf16[320,1280]{1,0:T(8,128)(2,1)}, ...) | async-done | bytes 4915216 | tf_op jit(solution)/shard_map/psum | solution.py:221
  (203 shorter events, 80.0 us)
Async XLA Ops:
  7.2 5.2 copy-start.3
  7.2 34.4 %all-gather.15.cloned.1.call-start = ((), (), s32[]{:S(2)}) async-start(), calls=%async_computation.11 | async-start | bytes 4096000 | tf_op jit(solution)/shard_map/all_gather | solution.py:55
  7.9 64.5 %all-gather.9.cloned.1.call-start = ((), (), s32[]{:S(2)}) async-start(), calls=%async_computation.8 | async-start | bytes 4096000 | tf_op jit(solution)/shard_map/all_gather | solution.py:56
  8.7 94.6 %all-gather.13.cloned.1.call-start = ((), (), s32[]{:S(2)}) async-start(), calls=%async_computation.10 | async-start | bytes 4096000 | tf_op jit(solution)/shard_map/all_gather | solution.py:54
  9.4 110.5 %all-gather.17.cloned.1.call-start = ((), (), s32[]{:S(2)}) async-start(), calls=%async_computation.12 | async-start | bytes 7864320 | tf_op jit(solution)/shard_map/all_gather | solution.py:80
  53.9 84.4 %all-gather.11.cloned.1.call-start = ((), (), s32[]{:S(2)}) async-start(), calls=%async_computation.9 | async-start | bytes 7864320 | tf_op jit(solution)/shard_map/all_gather | solution.py:81
  80.2 6.9 copy-start.44
  80.2 6.9 copy-start.25
  84.7 165.9 %all-gather.19.cloned.1.call-start = ((), (), s32[]{:S(2)}) async-start(), calls=%async_computation.13 | async-start | bytes 4096000 | tf_op jit(solution)/shard_map/all_gather | solution.py:57
  85.3 175.0 %all-gather.21.cloned.1.call-start = ((), (), s32[]{:S(2)}) async-start(), calls=%async_computation.14 | async-start | bytes 4096000 | tf_op jit(solution)/shard_map/all_gather | solution.py:58
  86.1 183.7 %all-gather.23.cloned.1.call-start = ((), (), s32[]{:S(2)}) async-start(), calls=%async_computation.15 | async-start | bytes 4096000 | tf_op jit(solution)/shard_map/all_gather | solution.py:59
  86.8 543.3 %reduce-scatter.11.cloned.1.call-start = ((), (), s32[]{:S(2)}) async-start(), calls=%async_computation.17 | async-start | bytes 15728640 | tf_op jit(solution)/shard_map/reduce_scatter | solution.py:175
  87.1 21.8 %copy-start.35 = (f32[80]{0:T(128)}, f32[80]{0:T(128)S(1)}, u32[]{:S(2)}) copy-start(f32[80]{0:T(128)S(1)} %fusion.51) | copy-start | bytes 964
  108.9 31.2 %copy-start.43 = (s32[2]{0:T(128)S(1)}, s32[2]{0:T(128)}, u32[]{:S(2)}) copy-start(s32[2]{0:T(128)} %param.19) | copy-start | bytes 28
  159.9 15.4 %copy-start.5 = (bf16[1,1024,1280]{1,2,0:T(8,128)(2,1)S(1)}, bf16[1,1024,1280]{1,2,0:T(8,128)(2,1)}, u32[]{:S(2)}) copy-start(bf16[1,1024,1280]{1,2,0:T(8,128)(2,1)} %get-tuple-element.330) | copy-start | bytes 7864324 | tf_op jit(solution)/shard_map/while
  159.9 15.4 %copy-start.8 = (bf16[2,512,16,80]{1,3,2,0:T(8,128)(2,1)S(1)}, bf16[2,512,16,80]{1,3,2,0:T(8,128)(2,1)}, u32[]{:S(2)}) copy-start(bf16[2,512,16,80]{1,3,2,0:T(8,128)(2,1)} %get-tuple-element.359) | copy-start | bytes 7864324 | tf_op jit(solution)/shard_map/while
  212.6 15.4 %copy-start.5 = (bf16[1,1024,1280]{1,2,0:T(8,128)(2,1)S(1)}, bf16[1,1024,1280]{1,2,0:T(8,128)(2,1)}, u32[]{:S(2)}) copy-start(bf16[1,1024,1280]{1,2,0:T(8,128)(2,1)} %get-tuple-element.330) | copy-start | bytes 7864324 | tf_op jit(solution)/shard_map/while
  212.6 15.4 %copy-start.8 = (bf16[2,512,16,80]{1,3,2,0:T(8,128)(2,1)S(1)}, bf16[2,512,16,80]{1,3,2,0:T(8,128)(2,1)}, u32[]{:S(2)}) copy-start(bf16[2,512,16,80]{1,3,2,0:T(8,128)(2,1)} %get-tuple-element.359) | copy-start | bytes 7864324 | tf_op jit(solution)/shard_map/while
  250.6 9.7 copy-start.31
  260.3 24.0 %copy-start.29 = (f32[1024]{0:T(1024)}, f32[1024]{0:T(1024)S(1)}, u32[]{:S(2)}) copy-start(f32[1024]{0:T(1024)S(1)} %get-tuple-element.206) | copy-start | bytes 12292
  260.3 9.4 copy-start.41
  269.7 10.1 copy-start.7
  269.7 10.1 copy-start.39
  279.8 4.5 copy-start.47
  279.8 4.5 copy-start.11
  284.3 4.3 copy-start.14
  286.2 2.4 copy-start.6
  311.2 6.5 copy-start
  311.2 6.4 copy-start.2
  438.3 8.8 copy-start.1
  447.2 6.4 copy-start
  447.2 6.4 copy-start.2
  574.2 8.8 copy-start.1
  583.4 56.1 %reduce-scatter.9.cloned.1.call-start = ((), (), s32[]{:S(2)}) async-start(), calls=%async_computation.16 | async-start | bytes 15728640 | tf_op jit(solution)/shard_map/reduce_scatter | solution.py:174
  583.5 1.7 copy-start.12
  583.5 1.7 copy-start.42
  584.0 10.3 copy-start.30
  584.0 10.3 copy-start.32
  584.0 82.9 %reduce-scatter.23.cloned.1.call-start = ((), (), s32[]{:S(2)}) async-start(), calls=%async_computation.23 | async-start | bytes 4096000 | tf_op jit(solution)/shard_map/reduce_scatter | solution.py:216
  594.2 11.6 %copy-start.10 = (bf16[160,8,2,512]{3,1,2,0:T(8,128)(2,1)S(1)}, bf16[160,8,2,512]{3,1,2,0:T(8,128)(2,1)}, u32[]{:S(2)}) copy-start(bf16[160,8,2,512]{3,1,2,0:T(8,128)(2,1)} %copy.65) | copy-start | bytes 7864324
  594.3 113.9 %reduce-scatter.21.cloned.1.call-start = ((), (), s32[]{:S(2)}) async-start(), calls=%async_computation.22 | async-start | bytes 4096000 | tf_op jit(solution)/shard_map/reduce_scatter | solution.py:213
  605.8 7.8 copy-start.36
  605.8 143.6 %reduce-scatter.19.cloned.1.call-start = ((), (), s32[]{:S(2)}) async-start(), calls=%async_computation.21 | async-start | bytes 4096000 | tf_op jit(solution)/shard_map/reduce_scatter | solution.py:210
  613.3 177.3 %reduce-scatter.13.cloned.1.call-start = ((), (), s32[]{:S(2)}) async-start(), calls=%async_computation.18 | async-start | bytes 4096000 | tf_op jit(solution)/shard_map/reduce_scatter | solution.py:201
  619.9 5.0 copy-start.16
  630.0 201.7 %reduce-scatter.17.cloned.1.call-start = ((), (), s32[]{:S(2)}) async-start(), calls=%async_computation.20 | async-start | bytes 4096000 | tf_op jit(solution)/shard_map/reduce_scatter | solution.py:207
  639.4 233.5 %reduce-scatter.15.cloned.1.call-start = ((), (), s32[]{:S(2)}) async-start(), calls=%async_computation.19 | async-start | bytes 4096000 | tf_op jit(solution)/shard_map/reduce_scatter | solution.py:204
  643.7 8.0 copy-start.28
  643.7 8.0 copy-start.13
  651.4 401.7 %all-reduce.4.cloned.1.call-start = ((), (), s32[]{:S(2)}) async-start(), calls=%async_computation.24 | async-start | bytes 9830400 | tf_op jit(solution)/shard_map/psum | solution.py:221
  652.2 220.7 %copy-start.40 = (f32[1280]{0:T(1024)S(1)}, f32[1280]{0:T(1024)}, u32[]{:S(2)}) copy-start(f32[1280]{0:T(1024)} %param.27) | copy-start | bytes 15364
  872.9 10.9 %copy-start.20 = (bf16[2,512,1280]{2,1,0:T(8,128)(2,1)S(1)}, bf16[2,512,1280]{2,1,0:T(8,128)(2,1)}, u32[]{:S(2)}) copy-start(bf16[2,512,1280]{2,1,0:T(8,128)(2,1)} %copy-done.19) | copy-start | bytes 7864324
  872.9 10.9 %copy-start.37 = (bf16[1280,1280]{1,0:T(8,128)(2,1)S(1)}, bf16[1280,1280]{1,0:T(8,128)(2,1)}, u32[]{:S(2)}) copy-start(bf16[1280,1280]{1,0:T(8,128)(2,1)} %all-gather.15.cloned.1.call-done) | copy-start | bytes 9830404
  883.8 3.6 copy-start.4
  883.8 3.6 copy-start.18
  883.8 3.6 copy-start.26
  883.9 3.6 copy-start.38
  883.9 5.0 copy-start.46
  888.9 6.3 copy-start.33
  888.9 6.3 copy-start.34
  1053.1 5.1 copy-start.24
  1053.1 6.3 copy-start.23
  1053.1 7.6 copy-start.22
  1055.7 6.3 copy-start.21
  (7 other events, 8.9 us)
Sparse Core Ops, SparseCore 0:
  9.6 31.9 all-gather.14
  43.1 29.2 all-gather.8
  74.0 29.2 all-gather.12
  104.7 15.2 all-gather.16
  121.9 16.3 all-gather.10
  139.7 30.4 all-gather.18
  171.7 29.2 all-gather.20
  202.6 29.2 all-gather.22
  583.5 19.3 reduce-scatter.10
  605.0 19.2 reduce-scatter.8
  626.9 39.9 reduce-scatter.22
  669.4 38.6 reduce-scatter.20
  710.7 38.6 reduce-scatter.18
  751.8 38.6 reduce-scatter.12
  793.0 38.6 reduce-scatter.16
  834.1 38.6 reduce-scatter.14
  877.1 175.9 all-reduce.3
where the time goes:
time: 1080 us; the launch traced here: 1070 us
  waiting for transfers between devices  401 us (37%)
  matrix products  357 us (33%)
  other arithmetic  131 us (12%)
  local copies, waits for them, and re-layouts  118 us (11%)
  blocking collectives  46.5 us (4%)
  between operations  14.7 us (1%)
    psum x1, waiting for transfers between devices, shards(): lax.psum(query_shard.astype(jnp.bfloat16), 'rep').astype(jnp.float32)  105 us
    dot_general x4, matrix products, masked_scores(): jnp.einsum('qhe,khe->hqk', queries, keys, preferred_element_type=jnp.floa...  57 us
    convert_element_type x2, other arithmetic, backward_one(): score_grad = (exact_prob * (prob_grad - row_inner)).astype(jnp.bfloat16)  55.7 us
    dot_general x2, matrix products, backward_one(): jnp.einsum('qhe,khe->hqk', grad_seq, values_heads, preferred_element_type...  51 us
    psum x1, blocking collectives, shards(): lax.psum((upbias_part, downbias_part, attngain_part, mlpgain_part, scale_...  46.5 us
    reduce_scatter x1, waiting for transfers between devices, shards(): lax.psum_scatter(output_part.astype(jnp.bfloat16), ('fsdp', 'ctx'), scatt...  41.3 us
    dynamic_update_slice x6, local copies, waits for them, and re-layouts, shards(): lax.map(backward_one, (queries, key_back, value_back, context_grad, logsu...  41.2 us
    reduce_scatter x1, waiting for transfers between devices, shards(): lax.psum_scatter(up_part.astype(jnp.bfloat16), ('fsdp', 'ctx'), scatter_d...  41.2 us
  transfers between devices with their start and end apart: 17, of which 12 were waited for; matrix products, arithmetic and copies ran while one was open for 25% of the time, Pallas kernels for 0%

commit v1 on v0

--- a/solution.py
+++ b/solution.py
@@ -7,6 +7,11 @@
 epsilon = 1e-06
 softplus_gain = 1.442695041
 masked_value = -1e30
+
+
+def gather_and_add(block, name):
+    pieces = lax.all_gather(block, name)
+    return jnp.sum(pieces, axis=0)
 
 
 def norm_factor(values):
@@ -218,7 +223,7 @@
         ).astype(jnp.float32),
     )
     query_total, key_total, value_total, output_total, up_total, down_total = (
-        lax.psum(query_shard.astype(jnp.bfloat16), "rep").astype(jnp.float32),
+        gather_and_add(query_shard.astype(jnp.bfloat16), "rep").astype(jnp.float32),
         lax.psum(key_shard.astype(jnp.bfloat16), "rep").astype(jnp.float32),
         lax.psum(value_shard.astype(jnp.bfloat16), "rep").astype(jnp.float32),
         lax.psum(output_shard.astype(jnp.bfloat16), "rep").astype(jnp.float32),

time: 1080 us -> 1160 us (1.074)
  waiting for transfers between devices: 401 us -> 483 us
    all_gather x0 -> x1, waiting for transfers between devices: none -> 96.3 us  [gather_and_add(): pieces = lax.all_gather(block, name)]
    reduce_scatter x1, waiting for transfers between devices: 6.04 us -> 29.5 us  [shards(): lax.psum_scatter(down_part.astype(jnp.bfloat16), ('fsdp', 'ctx'), scatter...]
    reduce_scatter x1, waiting for transfers between devices: 41.2 us -> 19.7 us  [shards(): lax.psum_scatter(query_part.astype(jnp.bfloat16), ('fsdp', 'ctx'), scatte...]
    psum x1, waiting for transfers between devices: 105 us -> 88.8 us  [shards(): lax.psum(key_shard.astype(jnp.bfloat16), 'rep').astype(jnp.float32)]
  transfers between devices with their start and end apart: 17 -> 18, of which waited for: 12 -> 13; matrix products, arithmetic and copies ran while one was open for 25% -> 24% of each run, Pallas kernels for 0% -> 0%
where the time goes in v1:
time: 1160 us; the launch traced here: 1150 us
  waiting for transfers between devices  483 us (42%)
  matrix products  359 us (31%)
  other arithmetic  132 us (11%)
  local copies, waits for them, and re-layouts  116 us (10%)
  blocking collectives  42.7 us (4%)
  between operations  15.1 us (1%)
    all_gather x1, waiting for transfers between devices, gather_and_add(): pieces = lax.all_gather(block, name)  96.3 us
    psum x1, waiting for transfers between devices, shards(): lax.psum(key_shard.astype(jnp.bfloat16), 'rep').astype(jnp.float32)  88.8 us
    dot_general x4, matrix products, masked_scores(): jnp.einsum('qhe,khe->hqk', queries, keys, preferred_element_type=jnp.floa...  56.9 us
    convert_element_type x2, other arithmetic, backward_one(): score_grad = (exact_prob * (prob_grad - row_inner)).astype(jnp.bfloat16)  55.7 us
    dot_general x2, matrix products, backward_one(): jnp.einsum('qhe,khe->hqk', grad_seq, values_heads, preferred_element_type...  50.9 us
    psum x1, blocking collectives, shards(): lax.psum((upbias_part, downbias_part, attngain_part, mlpgain_part, scale_...  42.7 us
    reduce_scatter x1, waiting for transfers between devices, shards(): lax.psum_scatter(up_part.astype(jnp.bfloat16), ('fsdp', 'ctx'), scatter_d...  41.3 us
    dynamic_update_slice x6, local copies, waits for them, and re-layouts, shards(): lax.map(backward_one, (queries, key_back, value_back, context_grad, logsu...  41.3 us
  transfers between devices with their start and end apart: 18, of which 13 were waited for; matrix products, arithmetic and copies ran while one was open for 24% of the time, Pallas kernels for 0%

profile of v1, /device:TPU:0, one launch (start us, length us, event | category | flops | bytes accessed | tf_op | source)
XLA Modules:
  0.0 1150.2 jit_solution(16950238218163220654)
XLA Ops:
  15.3 26.3 %all-gather.17.cloned.1.call-done = bf16[1280,1280]{1,0:T(8,128)(2,1)} async-done(((bf16[320,1280]{1,0:T(8,128)(2,1)}), bf16[1280,1280]{1,0:T(8,128)(2,1)}) %all-gather.17.cloned.1.call-update) | async-done | bytes 3276816 | tf_op jit(solution)/shard_map/all_gather | solution.py:60
  41.6 7.8 convolution_convert_fusion.5
  49.3 4.5 copy.37
  53.9 18.5 %all-gather.11.cloned.1.call-done = bf16[1280,1280]{1,0:T(8,128)(2,1)} async-done(((bf16[320,1280]{1,0:T(8,128)(2,1)}), bf16[1280,1280]{1,0:T(8,128)(2,1)}) %all-gather.11.cloned.1.call-update) | async-done | bytes 3276816 | tf_op jit(solution)/shard_map/all_gather | solution.py:61
  72.4 7.8 convolution_convert_fusion.6
  80.2 4.5 copy.35
  89.3 14.0 %all-gather.15.cloned.1.call-done = bf16[1280,1280]{1,0:T(8,128)(2,1)} async-done(((bf16[320,1280]{1,0:T(8,128)(2,1)}), bf16[1280,1280]{1,0:T(8,128)(2,1)}) %all-gather.15.cloned.1.call-update) | async-done | bytes 3276816 | tf_op jit(solution)/shard_map/all_gather | solution.py:59
  103.3 5.6 copy.36
  108.9 9.2 multiply_convert_fusion.4
  119.9 18.4 %all-gather.13.cloned.1.call-done = bf16[2,1024,1280]{1,2,0:T(8,128)(2,1)} async-done(((bf16[2,512,1280]{1,2,0:T(8,128)(2,1)}), bf16[2,1024,1280]{1,2,0:T(8,128)(2,1)}) %all-gather.13.cloned.1.call-update) | async-done | bytes 5242896 | tf_op jit(solution)/shard_map/all_gather | solution.py:86
  140.1 103.9 %while.26 = (s32[]{:T(128)}, bf16[2,512,16,80]{1,3,2,0:T(8,128)(2,1)}, f32[2,16,512,1]{2,1,3,0:T(8,128)S(1)}, bf16[2,1024,1280]{1,2,0:T(8,128)(2,1)}, s32[]{:T(1...) while((s32[]{:T(128)}, ...), condition=%wide.region_4.5_spmd, body=%wide.region_1.4_spmd.sunk | while | flops 2760893952 | bytes 154147024 | solution.py:106
  141.7 4.6 constant_dynamic-slice_fusion.7
  146.4 13.5 %select_reduce_fusion.2 = (f32[16,512]{1,0:T(8,128)S(1)}, f32[16,512,1024]{2,1,0:T(8,128)}) fusion(pred[512,1024]{1,0:T(8,128)(4,1)S(1)} %fusion.112, bf16[1024,16,80]{0,2,1:T(8,128)(2,1)S(1)} %bitcast.194, bf16[2,512,16,80]{1,3,2,0:T(8,128)(2,1)S(1)} %get-tuple-element.372, s32[]{:T(128)S(6)} %copy.79), kind=kOutput, calls=%fused_computation.2.clone.1 | convolution fusion | flops 1358946304 | bytes 38043652 | tf_op jit(solution)/shard_map/while/body/eval_jaxpr/qhe,khe->hqk/dot_general | solution.py:34
  159.9 15.4 %fusion.113 = f32[16,512]{1,0:T(8,128)S(1)} fusion(f32[16,512,1024]{2,1,0:T(8,128)} %get-tuple-element.331, f32[16,512]{1,0:T(8,128)S(1)} %get-tuple-element.332, pred[512,1024]{1,0:T(8,128)(4,1)S(1)} %fusion.112), kind=kLoop, calls=%fused_computation.3.clone.1 | loop fusion | flops 25157632 | bytes 34144256 | tf_op jit(solution)/shard_map/while/body/eval_jaxpr/reduce_sum | solution.py:96
  175.3 15.2 %bitcast_dynamic-update-slice_fusion.6 = bf16[2,512,16,80]{1,3,2,0:T(8,128)(2,1)S(1)} fusion(bf16[2,512,16,80]{1,3,2,0:T(8,128)(2,1)S(1)} %copy-done.8, s32[]{:T(128)S(6)} %copy.79, bf16[1024,16,80]{0,2,1:T(8,128)(2,1)S(1)} %bitcast.197, f32[16,512,1024]{2,1,0:T(8,128)} %get-tuple-element.331, f32[16,512]{1,0:T(8,128)S(1)} %fusion.113, ...), kind=kOutput, calls=%fused_computation.5.clone.1 | convolution fusion | flops 1375731712 | bytes 39387140 | tf_op jit(solution)/shard_map/while/body/eval_jaxpr/hqk,khe->qhe/dot_general | solution.py:98
  193.7 4.6 constant_dynamic-slice_fusion.7
  198.3 14.3 %select_reduce_fusion.2 = (f32[16,512]{1,0:T(8,128)S(1)}, f32[16,512,1024]{2,1,0:T(8,128)}) fusion(pred[512,1024]{1,0:T(8,128)(4,1)S(1)} %fusion.112, bf16[1024,16,80]{0,2,1:T(8,128)(2,1)S(1)} %bitcast.194, bf16[2,512,16,80]{1,3,2,0:T(8,128)(2,1)S(1)} %get-tuple-element.372, s32[]{:T(128)S(6)} %copy.79), kind=kOutput, calls=%fused_computation.2.clone.1 | convolution fusion | flops 1358946304 | bytes 38043652 | tf_op jit(solution)/shard_map/while/body/eval_jaxpr/qhe,khe->hqk/dot_general | solution.py:34
  212.6 15.3 %fusion.113 = f32[16,512]{1,0:T(8,128)S(1)} fusion(f32[16,512,1024]{2,1,0:T(8,128)} %get-tuple-element.331, f32[16,512]{1,0:T(8,128)S(1)} %get-tuple-element.332, pred[512,1024]{1,0:T(8,128)(4,1)S(1)} %fusion.112), kind=kLoop, calls=%fused_computation.3.clone.1 | loop fusion | flops 25157632 | bytes 34144256 | tf_op jit(solution)/shard_map/while/body/eval_jaxpr/reduce_sum | solution.py:96
  228.0 14.3 %bitcast_dynamic-update-slice_fusion.6 = bf16[2,512,16,80]{1,3,2,0:T(8,128)(2,1)S(1)} fusion(bf16[2,512,16,80]{1,3,2,0:T(8,128)(2,1)S(1)} %copy-done.8, s32[]{:T(128)S(6)} %copy.79, bf16[1024,16,80]{0,2,1:T(8,128)(2,1)S(1)} %bitcast.197, f32[16,512,1024]{2,1,0:T(8,128)} %get-tuple-element.331, f32[16,512]{1,0:T(8,128)S(1)} %fusion.113, ...), kind=kOutput, calls=%fused_computation.5.clone.1 | convolution fusion | flops 1375731712 | bytes 39387140 | tf_op jit(solution)/shard_map/while/body/eval_jaxpr/hqk,khe->qhe/dot_general | solution.py:98
  250.6 9.7 multiply_reduce_fusion.3
  260.4 9.4 fusion.54
  269.8 10.1 convert_reduce_fusion.1
  288.6 4.9 convolution_convert_fusion.4
  293.5 8.5 reshape.300
  302.0 7.2 copy.40
  311.1 272.3 %while.27 = (s32[]{:T(128)}, bf16[2,512,16,80]{1,3,2,0:T(8,128)(2,1)}, f32[2,1024,1280]{2,1,0:T(8,128)}, f32[2,1024,1280]{2,1,0:T(8,128)}, bf16[2,1024,1280]{1,2...) while((s32[]{:T(128)}, ...), condition=%wide.region_9.10_spmd, body=%wide.region_7.9_spmd.sunk | while | flops 6812591616 | bytes 374577376 | solution.py:175
  317.9 14.5 %fusion.123 = f32[16,512,1024]{2,1,0:T(8,128)} fusion(bf16[1024,16,80]{0,2,1:T(8,128)(2,1)S(1)} %bitcast.191, bf16[2,512,16,80]{1,3,2,0:T(8,128)(2,1)} %copy-done, s32[]{:T(128)S(6)} %copy.89), kind=kOutput, calls=%fused_computation.34.clone.1 | convolution fusion | flops 1342177280 | bytes 37486596 | tf_op jit(solution)/shard_map/while/body/eval_jaxpr/qhe,khe->hqk/dot_general | solution.py:34
  332.4 17.1 %fusion.125 = f32[16,80,1024]{2,1,0:T(8,128)} fusion(f32[16,512,1024]{2,1,0:T(8,128)} %fusion.123, f32[16,512]{1,0:T(8,128)S(1)} %dynamic-slice_bitcast_fusion.2, pred[512,1024]{1,0:T(8,128)(4,1)S(1)} %fusion.124, bf16[2,512,16,80]{1,3,2,0:T(8,128)(2,1)} %get-tuple-element.408, s32[]{:T(128)S(6)} %copy.89), kind=kOutput, calls=%fused_computation.22.clone.1 | convolution fusion | flops 1367343104 | bytes 40665092 | tf_op jit(solution)/shard_map/while/body/eval_jaxpr/hqk,qhe->khe/dot_general | solution.py:166
  349.5 5.9 copy.69
  355.4 25.4 %multiply_reduce_fusion.5 = (f32[16,512]{1,0:T(8,128)S(1)}, f32[16,512,1024]{2,1,0:T(8,128)}) fusion(f32[16,512,1024]{2,1,0:T(8,128)} %fusion.123, f32[16,512]{1,0:T(8,128)S(1)} %dynamic-slice_bitcast_fusion.2, pred[512,1024]{1,0:T(8,128)(4,1)S(1)} %fusion.124, bf16[1024,16,80]{0,2,1:T(8,128)(2,1)} %bitcast.196, ...), kind=kOutput, calls=%fused_computation.19.clone.1 | convolution fusion | flops 1375723520 | bytes 71630848 | tf_op jit(solution)/shard_map/while/body/eval_jaxpr/qhe,khe->hqk/dot_general | solution.py:155
  380.8 27.8 %multiply_convert_fusion.10 = bf16[16,512,1024]{2,1,0:T(8,128)(2,1)} fusion(f32[16,512,1024]{2,1,0:T(8,128)} %get-tuple-element.344, f32[16,512,1024]{2,1,0:T(8,128)} %fusion.123, f32[16,512]{1,0:T(8,128)S(1)} %get-tuple-element.345, f32[16,512]{1,0:T(8,128)S(1)} %dynamic-slice_bitcast_fusion.2, pred[512,1024]{1,0:T(8,128)(4,1)S(1)} %fusion.124), kind=kLoop, calls=%fused_computation.18.clone.1 | loop fusion | flops 41943040 | bytes 84475904 | tf_op jit(solution)/shard_map/while/body/eval_jaxpr/convert_element_type | solution.py:159
  408.7 12.1 %bitcast_dynamic-update-slice_fusion.8 = bf16[2,512,16,80]{1,3,2,0:T(8,128)(2,1)} fusion(bf16[2,512,16,80]{1,3,2,0:T(8,128)(2,1)} %get-tuple-element.388, s32[]{:T(128)S(6)} %copy.89, bf16[1024,16,80]{0,2,1:T(8,128)(2,1)S(1)} %bitcast.192, bf16[16,512,1024]{2,1,0:T(8,128)(2,1)} %multiply_convert_fusion.10), kind=kOutput, calls=%fused_computation.26.clone.1 | convolution fusion | flops 1342177280 | bytes 22020100 | tf_op jit(solution)/shard_map/while/body/eval_jaxpr/hqk,khe->qhe/dot_general | solution.py:160
  420.8 11.6 %fusion.126 = f32[16,80,1024]{2,1,0:T(8,128)} fusion(bf16[16,512,1024]{2,1,0:T(8,128)(2,1)} %multiply_convert_fusion.10, bf16[2,512,16,80]{1,3,2,0:T(8,128)(2,1)} %copy-done, s32[]{:T(128)S(6)} %copy.89), kind=kOutput, calls=%fused_computation.32.clone.1 | convolution fusion | flops 1342177280 | bytes 23330820 | tf_op jit(solution)/shard_map/while/body/eval_jaxpr/hqk,qhe->khe/dot_general | solution.py:163
  432.4 5.9 copy.70
  438.3 8.8 constant_dynamic-update-slice_fusion.3
  453.8 14.5 %fusion.123 = f32[16,512,1024]{2,1,0:T(8,128)} fusion(bf16[1024,16,80]{0,2,1:T(8,128)(2,1)S(1)} %bitcast.191, bf16[2,512,16,80]{1,3,2,0:T(8,128)(2,1)} %copy-done, s32[]{:T(128)S(6)} %copy.89), kind=kOutput, calls=%fused_computation.34.clone.1 | convolution fusion | flops 1342177280 | bytes 37486596 | tf_op jit(solution)/shard_map/while/body/eval_jaxpr/qhe,khe->hqk/dot_general | solution.py:34
  468.3 17.1 %fusion.125 = f32[16,80,1024]{2,1,0:T(8,128)} fusion(f32[16,512,1024]{2,1,0:T(8,128)} %fusion.123, f32[16,512]{1,0:T(8,128)S(1)} %dynamic-slice_bitcast_fusion.2, pred[512,1024]{1,0:T(8,128)(4,1)S(1)} %fusion.124, bf16[2,512,16,80]{1,3,2,0:T(8,128)(2,1)} %get-tuple-element.408, s32[]{:T(128)S(6)} %copy.89), kind=kOutput, calls=%fused_computation.22.clone.1 | convolution fusion | flops 1367343104 | bytes 40665092 | tf_op jit(solution)/shard_map/while/body/eval_jaxpr/hqk,qhe->khe/dot_general | solution.py:166
  485.4 5.9 copy.69
  491.3 25.4 %multiply_reduce_fusion.5 = (f32[16,512]{1,0:T(8,128)S(1)}, f32[16,512,1024]{2,1,0:T(8,128)}) fusion(f32[16,512,1024]{2,1,0:T(8,128)} %fusion.123, f32[16,512]{1,0:T(8,128)S(1)} %dynamic-slice_bitcast_fusion.2, pred[512,1024]{1,0:T(8,128)(4,1)S(1)} %fusion.124, bf16[1024,16,80]{0,2,1:T(8,128)(2,1)} %bitcast.196, ...), kind=kOutput, calls=%fused_computation.19.clone.1 | convolution fusion | flops 1375723520 | bytes 71630848 | tf_op jit(solution)/shard_map/while/body/eval_jaxpr/qhe,khe->hqk/dot_general | solution.py:155
  516.7 27.8 %multiply_convert_fusion.10 = bf16[16,512,1024]{2,1,0:T(8,128)(2,1)} fusion(f32[16,512,1024]{2,1,0:T(8,128)} %get-tuple-element.344, f32[16,512,1024]{2,1,0:T(8,128)} %fusion.123, f32[16,512]{1,0:T(8,128)S(1)} %get-tuple-element.345, f32[16,512]{1,0:T(8,128)S(1)} %dynamic-slice_bitcast_fusion.2, pred[512,1024]{1,0:T(8,128)(4,1)S(1)} %fusion.124), kind=kLoop, calls=%fused_computation.18.clone.1 | loop fusion | flops 41943040 | bytes 84475904 | tf_op jit(solution)/shard_map/while/body/eval_jaxpr/convert_element_type | solution.py:159
  544.6 12.0 %bitcast_dynamic-update-slice_fusion.8 = bf16[2,512,16,80]{1,3,2,0:T(8,128)(2,1)} fusion(bf16[2,512,16,80]{1,3,2,0:T(8,128)(2,1)} %get-tuple-element.388, s32[]{:T(128)S(6)} %copy.89, bf16[1024,16,80]{0,2,1:T(8,128)(2,1)S(1)} %bitcast.192, bf16[16,512,1024]{2,1,0:T(8,128)(2,1)} %multiply_convert_fusion.10), kind=kOutput, calls=%fused_computation.26.clone.1 | convolution fusion | flops 1342177280 | bytes 22020100 | tf_op jit(solution)/shard_map/while/body/eval_jaxpr/hqk,khe->qhe/dot_general | solution.py:160
  556.6 11.6 %fusion.126 = f32[16,80,1024]{2,1,0:T(8,128)} fusion(bf16[16,512,1024]{2,1,0:T(8,128)(2,1)} %multiply_convert_fusion.10, bf16[2,512,16,80]{1,3,2,0:T(8,128)(2,1)} %copy-done, s32[]{:T(128)S(6)} %copy.89), kind=kOutput, calls=%fused_computation.32.clone.1 | convolution fusion | flops 1342177280 | bytes 23330820 | tf_op jit(solution)/shard_map/while/body/eval_jaxpr/hqk,qhe->khe/dot_general | solution.py:163
  568.2 5.9 copy.70
  574.1 8.8 constant_dynamic-update-slice_fusion.3
  593.8 5.1 convolution_convert_fusion.3
  599.0 10.0 convolution_convert_fusion
  609.3 9.9 convolution_convert_fusion.1
  619.3 8.8 convolution_convert_fusion.2
  632.5 5.1 fusion.32
  642.0 5.1 fusion.31
  647.2 19.7 %reduce-scatter.13.cloned.1.call-done = bf16[320,1280]{1,0:T(8,128)(2,1)} async-done(((bf16[1280,1280]{1,0:T(8,128)(2,1)}), bf16[320,1280]{1,0:T(8,128)(2,1)}) %reduce-scatter.13.cloned.1.call-update) | async-done | bytes 819216 | tf_op jit(solution)/shard_map/reduce_scatter | solution.py:206
  667.7 10.9 add_convert_fusion
  678.6 29.5 %reduce-scatter.23.cloned.1.call-done = bf16[320,1280]{1,0:T(8,128)(2,1)} async-done(((bf16[1280,1280]{1,0:T(8,128)(2,1)}), bf16[320,1280]{1,0:T(8,128)(2,1)}) %reduce-scatter.23.cloned.1.call-update) | async-done | bytes 819216 | tf_op jit(solution)/shard_map/reduce_scatter | solution.py:221
  708.1 41.3 %reduce-scatter.21.cloned.1.call-done = bf16[320,1280]{1,0:T(8,128)(2,1)} async-done(((bf16[1280,1280]{1,0:T(8,128)(2,1)}), bf16[320,1280]{1,0:T(8,128)(2,1)}) %reduce-scatter.21.cloned.1.call-update) | async-done | bytes 819216 | tf_op jit(solution)/shard_map/reduce_scatter | solution.py:218
  749.4 41.2 %reduce-scatter.19.cloned.1.call-done = bf16[320,1280]{1,0:T(8,128)(2,1)} async-done(((bf16[1280,1280]{1,0:T(8,128)(2,1)}), bf16[320,1280]{1,0:T(8,128)(2,1)}) %reduce-scatter.19.cloned.1.call-update) | async-done | bytes 819216 | tf_op jit(solution)/shard_map/reduce_scatter | solution.py:215
  790.6 41.2 %reduce-scatter.17.cloned.1.call-done = bf16[320,1280]{1,0:T(8,128)(2,1)} async-done(((bf16[1280,1280]{1,0:T(8,128)(2,1)}), bf16[320,1280]{1,0:T(8,128)(2,1)}) %reduce-scatter.17.cloned.1.call-update) | async-done | bytes 819216 | tf_op jit(solution)/shard_map/reduce_scatter | solution.py:212
  831.7 41.2 %reduce-scatter.15.cloned.1.call-done = bf16[320,1280]{1,0:T(8,128)(2,1)} async-done(((bf16[1280,1280]{1,0:T(8,128)(2,1)}), bf16[320,1280]{1,0:T(8,128)(2,1)}) %reduce-scatter.15.cloned.1.call-update) | async-done | bytes 819216 | tf_op jit(solution)/shard_map/reduce_scatter | solution.py:209
  872.9 7.6 fusion.55
  880.6 96.3 %all-gather.27.cloned.1.call-done = bf16[2560,1280]{1,0:T(8,128)(2,1)} async-done(((bf16[320,1280]{1,0:T(8,128)(2,1)}), bf16[2560,1280]{1,0:T(8,128)(2,1)}) %all-gather.27.cloned.1.call-update) | async-done | bytes 6553616 | tf_op jit(solution)/shard_map/all_gather | solution.py:13
  982.4 7.8 fusion.56
  990.3 6.6 fusion.46
  996.9 42.7 %all-reduce = (f32[1280]{0:T(1024)}, f32[1280]{0:T(1024)}, f32[1280]{0:T(1024)}, f32[1280]{0:T(1024)}, f32[80]{0:T(128)}) all-reduce(f32[1280]{0:T(1024)S(1)} %copy-done.34, f32[1280]{0:T(1024)S(1)} %convert_reduce_fusion, f32[1280]{0:T(1024)S(1)} %get-tuple-element.144, ...), channel_id=1, replica_groups=mesh['rep'=8,'fsdp'=2,'ctx'=2] {'rep','fsdp','ctx'}, use_global_device_ids=true, to_apply=%region_24.25 | all-reduce | flops 5200 | bytes 41600 | tf_op jit(solution)/shard_map/psum | solution.py:233
  1039.6 5.9 fusion.43
  1045.5 88.8 %all-reduce.4.cloned.1.call-done = (bf16[320,1280]{1,0:T(8,128)(2,1)}, bf16[320,1280]{1,0:T(8,128)(2,1)}, bf16[320,1280]{1,0:T(8,128)(2,1)}, bf16[320,1280]{1,0:T(8,128)(2,1)}, bf16[320,1280]{1,0:T(8,128)(2,1)}) async-done(((bf16[320,1280]{1,0:T(8,128)(2,1)}, bf16[320,1280]{1,0:T(8,128)(2,1)}, bf16[320,1280]{1,0:T(8,128)(2,1)}, bf16[320,1280]{1,0:T(8,128)(2,1)}, bf16[320,1280]{1,0:T(8,128)(2,1)}), ...) | async-done | bytes 4096016 | tf_op jit(solution)/shard_map/psum | solution.py:227
  (210 shorter events, 87.7 us)
Async XLA Ops:
  7.2 5.2 copy-start.3
  7.2 34.4 %all-gather.17.cloned.1.call-start = ((), (), s32[]{:S(2)}) async-start(), calls=%async_computation.11 | async-start | bytes 4096000 | tf_op jit(solution)/shard_map/all_gather | solution.py:60
  7.9 64.5 %all-gather.11.cloned.1.call-start = ((), (), s32[]{:S(2)}) async-start(), calls=%async_computation.8 | async-start | bytes 4096000 | tf_op jit(solution)/shard_map/all_gather | solution.py:61
  8.7 94.6 %all-gather.15.cloned.1.call-start = ((), (), s32[]{:S(2)}) async-start(), calls=%async_computation.10 | async-start | bytes 4096000 | tf_op jit(solution)/shard_map/all_gather | solution.py:59
  9.4 110.5 %all-gather.19.cloned.1.call-start = ((), (), s32[]{:S(2)}) async-start(), calls=%async_computation.12 | async-start | bytes 7864320 | tf_op jit(solution)/shard_map/all_gather | solution.py:85
  53.9 84.4 %all-gather.13.cloned.1.call-start = ((), (), s32[]{:S(2)}) async-start(), calls=%async_computation.9 | async-start | bytes 7864320 | tf_op jit(solution)/shard_map/all_gather | solution.py:86
  80.2 6.9 copy-start.44
  80.2 6.9 copy-start.26
  84.7 165.9 %all-gather.21.cloned.1.call-start = ((), (), s32[]{:S(2)}) async-start(), calls=%async_computation.13 | async-start | bytes 4096000 | tf_op jit(solution)/shard_map/all_gather | solution.py:62
  85.3 175.0 %all-gather.23.cloned.1.call-start = ((), (), s32[]{:S(2)}) async-start(), calls=%async_computation.14 | async-start | bytes 4096000 | tf_op jit(solution)/shard_map/all_gather | solution.py:63
  86.1 183.7 %all-gather.25.cloned.1.call-start = ((), (), s32[]{:S(2)}) async-start(), calls=%async_computation.15 | async-start | bytes 4096000 | tf_op jit(solution)/shard_map/all_gather | solution.py:64
  86.8 541.3 %reduce-scatter.11.cloned.1.call-start = ((), (), s32[]{:S(2)}) async-start(), calls=%async_computation.17 | async-start | bytes 15728640 | tf_op jit(solution)/shard_map/reduce_scatter | solution.py:180
  87.1 21.8 %copy-start.36 = (f32[80]{0:T(128)}, f32[80]{0:T(128)S(1)}, u32[]{:S(2)}) copy-start(f32[80]{0:T(128)S(1)} %fusion.51) | copy-start | bytes 964
  108.9 31.2 %copy-start.43 = (s32[2]{0:T(128)S(1)}, s32[2]{0:T(128)}, u32[]{:S(2)}) copy-start(s32[2]{0:T(128)} %param.19) | copy-start | bytes 28
  159.9 15.4 %copy-start.5 = (bf16[1,1024,1280]{1,2,0:T(8,128)(2,1)S(1)}, bf16[1,1024,1280]{1,2,0:T(8,128)(2,1)}, u32[]{:S(2)}) copy-start(bf16[1,1024,1280]{1,2,0:T(8,128)(2,1)} %get-tuple-element.329) | copy-start | bytes 7864324 | tf_op jit(solution)/shard_map/while
  159.9 15.4 %copy-start.8 = (bf16[2,512,16,80]{1,3,2,0:T(8,128)(2,1)S(1)}, bf16[2,512,16,80]{1,3,2,0:T(8,128)(2,1)}, u32[]{:S(2)}) copy-start(bf16[2,512,16,80]{1,3,2,0:T(8,128)(2,1)} %get-tuple-element.358) | copy-start | bytes 7864324 | tf_op jit(solution)/shard_map/while
  212.6 15.4 %copy-start.5 = (bf16[1,1024,1280]{1,2,0:T(8,128)(2,1)S(1)}, bf16[1,1024,1280]{1,2,0:T(8,128)(2,1)}, u32[]{:S(2)}) copy-start(bf16[1,1024,1280]{1,2,0:T(8,128)(2,1)} %get-tuple-element.329) | copy-start | bytes 7864324 | tf_op jit(solution)/shard_map/while
  212.6 15.4 %copy-start.8 = (bf16[2,512,16,80]{1,3,2,0:T(8,128)(2,1)S(1)}, bf16[2,512,16,80]{1,3,2,0:T(8,128)(2,1)}, u32[]{:S(2)}) copy-start(bf16[2,512,16,80]{1,3,2,0:T(8,128)(2,1)} %get-tuple-element.358) | copy-start | bytes 7864324 | tf_op jit(solution)/shard_map/while
  250.6 9.8 copy-start.32
  260.3 24.0 %copy-start.30 = (f32[1024]{0:T(1024)}, f32[1024]{0:T(1024)S(1)}, u32[]{:S(2)}) copy-start(f32[1024]{0:T(1024)S(1)} %get-tuple-element.205) | copy-start | bytes 12292
  260.4 9.4 copy-start.41
  269.8 10.1 copy-start.7
  269.8 10.1 copy-start.39
  279.8 4.5 copy-start.46
  279.8 4.5 copy-start.12
  284.3 4.3 copy-start.16
  311.2 6.5 copy-start
  311.2 6.4 copy-start.2
  438.3 8.8 copy-start.1
  447.1 6.4 copy-start
  447.1 6.4 copy-start.2
  574.1 8.8 copy-start.1
  583.3 54.4 %reduce-scatter.9.cloned.1.call-start = ((), (), s32[]{:S(2)}) async-start(), calls=%async_computation.16 | async-start | bytes 15728640 | tf_op jit(solution)/shard_map/reduce_scatter | solution.py:179
  583.9 83.0 %reduce-scatter.13.cloned.1.call-start = ((), (), s32[]{:S(2)}) async-start(), calls=%async_computation.18 | async-start | bytes 4096000 | tf_op jit(solution)/shard_map/reduce_scatter | solution.py:206
  588.9 4.9 copy-start.18
  593.8 5.2 copy-start.13
  593.8 5.2 copy-start.42
  599.0 10.3 copy-start.31
  599.0 10.3 copy-start.33
  599.0 109.1 %reduce-scatter.23.cloned.1.call-start = ((), (), s32[]{:S(2)}) async-start(), calls=%async_computation.23 | async-start | bytes 4096000 | tf_op jit(solution)/shard_map/reduce_scatter | solution.py:221
  609.0 10.2 copy-start.10
  609.0 140.3 %reduce-scatter.21.cloned.1.call-start = ((), (), s32[]{:S(2)}) async-start(), calls=%async_computation.22 | async-start | bytes 4096000 | tf_op jit(solution)/shard_map/reduce_scatter | solution.py:218
  619.2 171.4 %reduce-scatter.19.cloned.1.call-start = ((), (), s32[]{:S(2)}) async-start(), calls=%async_computation.21 | async-start | bytes 4096000 | tf_op jit(solution)/shard_map/reduce_scatter | solution.py:215
  628.0 4.5 copy-start.19
  628.1 203.7 %reduce-scatter.17.cloned.1.call-start = ((), (), s32[]{:S(2)}) async-start(), calls=%async_computation.20 | async-start | bytes 4096000 | tf_op jit(solution)/shard_map/reduce_scatter | solution.py:212
  637.6 235.3 %reduce-scatter.15.cloned.1.call-start = ((), (), s32[]{:S(2)}) async-start(), calls=%async_computation.19 | async-start | bytes 4096000 | tf_op jit(solution)/shard_map/reduce_scatter | solution.py:209
  642.0 25.2 %copy-start.29 = (f32[1,4,2,128]{3,1,2,0:T(4,128)S(1)}, f32[1,4,2,128]{3,1,2,0:T(4,128)}, u32[]{:S(2)}) copy-start(f32[1,4,2,128]{3,1,2,0:T(4,128)} %copy-done.28) | copy-start | bytes 12292
  647.2 20.1 %copy-start.14 = (bf16[2,512,1280]{2,1,0:T(8,128)(2,1)S(1)}, bf16[2,512,1280]{2,1,0:T(8,128)(2,1)}, u32[]{:S(2)}) copy-start(bf16[2,512,1280]{2,1,0:T(8,128)(2,1)} %param.31) | copy-start | bytes 7864324
  647.2 20.5 %copy-start.45 = (f32[80]{0:T(128)S(1)}, f32[80]{0:T(128)}, u32[]{:S(2)}) copy-start(f32[80]{0:T(128)} %param.30) | copy-start | bytes 964
  647.2 20.5 %copy-start.40 = (f32[1280]{0:T(1024)S(1)}, f32[1280]{0:T(1024)}, u32[]{:S(2)}) copy-start(f32[1280]{0:T(1024)} %param.27) | copy-start | bytes 15364
  647.2 329.7 %all-gather.27.cloned.1.call-start = ((), (), s32[]{:S(2)}) async-start(), calls=%async_computation.24 | async-start | bytes 7372800 | tf_op jit(solution)/shard_map/all_gather | solution.py:13
  666.9 467.4 %all-reduce.4.cloned.1.call-start = ((), (), s32[]{:S(2)}) async-start(), calls=%async_computation.25 | async-start | bytes 8192000 | tf_op jit(solution)/shard_map/psum | solution.py:227
  667.7 205.3 %copy-start.15 = (bf16[1280,1280]{1,0:T(8,128)(2,1)S(1)}, bf16[1280,1280]{1,0:T(8,128)(2,1)}, u32[]{:S(2)}) copy-start(bf16[1280,1280]{1,0:T(8,128)(2,1)} %all-gather.15.cloned.1.call-done) | copy-start | bytes 9830404
  981.1 9.1 slice-start
  982.4 7.9 copy-start.4
  982.4 7.9 copy-start.21
  982.4 7.9 copy-start.27
  982.4 7.9 copy-start.38
  982.4 7.9 slice-start.1
  990.3 6.6 copy-start.34
  990.3 6.6 copy-start.35
  1134.3 5.0 copy-start.25
  1134.3 6.3 copy-start.24
  1134.3 7.5 copy-start.23
  (9 other events, 13.9 us)
Sparse Core Ops, SparseCore 0:
  9.6 31.9 all-gather.16
  43.1 29.2 all-gather.10
  74.0 29.2 all-gather.14
  104.7 15.2 all-gather.18
  121.9 16.3 all-gather.12
  139.7 30.4 all-gather.20
  171.7 29.2 all-gather.22
  202.6 29.2 all-gather.24
  583.5 19.2 reduce-scatter.10
  604.9 19.2 reduce-scatter.8
  626.9 40.0 reduce-scatter.12
  669.3 38.6 reduce-scatter.22
  710.6 38.7 reduce-scatter.20
  751.8 38.7 reduce-scatter.18
  793.0 38.7 reduce-scatter.16
  834.2 38.6 reduce-scatter.14
  874.9 101.8 all-gather.26
  981.0 153.2 all-reduce.3
